TPU v7x, 32 devices: a whole 2x2x4 slice. The times are simulated.
32 devices in a mesh: role: 2 (over core), wide: 4 (over y, x), tp: 4 (over z).
Axes of the slice: x: 2, y: 2, z: 4, core: 2. Of those that a mesh axis runs over, the one named last changes fastest.
Arguments:
- normed: bfloat16 [2048, 4096], P('wide', ('role', 'tp')), may hold values from -0.29882812 to 0.29882812
- queries: bfloat16 [2048, 4096], P('wide', 'tp'), may hold values from -4 to 4
- keys: bfloat16 [2048, 1024], P('wide'), may hold values from -4 to 4
- values: bfloat16 [2048, 1024], P('wide'), may hold values from -6 to 6
- attn_out: bfloat16 [2048, 4096], P('wide', 'tp'), may hold values from -0.29882812 to 0.29882812
- row_logsumexp: float32 [32, 2048], P('tp'), as said below
- out_grad: bfloat16 [2048, 4096], P('wide', ('role', 'tp')), may hold values from -6 to 6
- out_weight: bfloat16 [4096, 4096], P('tp'), may hold values from -0.09375 to 0.09375
- qkv_weight: bfloat16 [4096, 6144], P(('role', 'tp')), may hold values from -0.09375 to 0.09375
- documents: int32 [2048], replicated, may hold values from 0 to 2, as said below
- tasks: int32 [4, 8, 2], replicated, may hold values from -1 to 7, as said below
Outputs:
- normed_grad: bfloat16 [2048, 4096], P('wide', ('role', 'tp'))
- out_weight_grad: bfloat16 [4096, 4096], P('tp', ('role', 'wide'))
- qkv_weight_grad: bfloat16 [4096, 6144], P(('role', 'tp'), 'wide')
Inputs may be any that keep to these rules, and one draw needn't show every extreme that they name: `documents`: document numbers never fall along the tokens, and every number from 0 to 2 is used. `tasks`: row s lists in its first slots the query blocks of server s, in [s, j, 0], followed by slots holding -1 in both places; every query block from 0 to 7 stands in exactly one slot of the table; [s, j, 1] is the block holding the first token of the document of the query block's first token. row_logsumexp[h, i] is the logarithm of the sum, over the tokens j that token i may attend, of exp(scores[h, i, j]) as computed from queries and keys.
All inputs are finite; a program needn't handle non-finite values.
Results may differ from a plain program's by a relative error of at most 0.018.
Values may be sent and summed in bfloat16 or wider, within the bound.
No kernel may reach another device: no remote copies, remote signals or barrier semaphores. Data moves between devices by JAX's collectives and lax.ppermute only.
A program may use at most 128 MiB of HBM per device.

v0:
```python
import jax
import jax.numpy as jnp
from jax import lax
from jax.sharding import PartitionSpec as P

D = 4096
QUERY_HEADS = 32
KEY_VALUE_HEADS = 8
HEAD_SIZE = 128


def local(
    normed,
    queries,
    keys,
    values,
    attn_out,
    row_logsumexp,
    out_grad,
    out_weight,
    qkv_weight,
    documents,
    tasks,
):
    role_pos = lax.axis_index("role")
    is_worker = role_pos == 0
    wide_count = lax.axis_size("wide")
    wide_pos = lax.axis_index("wide")
    tp_pos = lax.axis_index("tp")
    local_rows = normed.shape[0]
    row_halves = local_rows // 2
    head_count = queries.shape[1] // HEAD_SIZE
    pair_count = head_count // 2
    kv_count = max(1, head_count // 4)
    score_scale = HEAD_SIZE ** (-0.5)
    total_rows = wide_count * local_rows
    block_count = tasks.shape[1]
    full_grad = lax.all_gather(out_grad, ("role", "tp"), axis=1, tiled=True)
    grad_half = lax.dynamic_slice_in_dim(full_grad, role_pos * (D // 2), D // 2, 1)
    out_part = lax.dot_general(
        attn_out, grad_half, (((0,), (0,)), ((), ())), preferred_element_type=jnp.float32
    )

    def worker_side():
        return lax.dot_general(
            full_grad, out_weight, (((1,), (1,)), ((), ())), preferred_element_type=jnp.float32
        ).astype(jnp.bfloat16)

    def server_side():
        return queries

    first_piece = lax.cond(is_worker, worker_side, server_side)
    kv_start = tp_pos * head_count // 4 * HEAD_SIZE
    key_cols = lax.dynamic_slice_in_dim(keys, kv_start, kv_count * HEAD_SIZE, 1)
    value_cols = lax.dynamic_slice_in_dim(values, kv_start, kv_count * HEAD_SIZE, 1)
    kv_piece = jnp.where(is_worker, key_cols, value_cols)
    out_piece = lax.dynamic_slice_in_dim(
        attn_out, role_pos * pair_count * HEAD_SIZE, pair_count * HEAD_SIZE, 1
    )
    gathered = (
        lax.all_gather(first_piece, ("role", "wide"), axis=0, tiled=True),
        lax.all_gather(kv_piece, ("role", "wide"), axis=0, tiled=True),
        lax.all_gather(out_piece, ("role", "wide"), axis=0, tiled=True),
    )
    grad_all = gathered[0][:total_rows]
    query_all = gathered[0][total_rows:]
    key_all = gathered[1][:total_rows]
    value_all = gathered[1][total_rows:]
    output_all = gathered[2].reshape(2, total_rows, pair_count, HEAD_SIZE)
    delta_all = jnp.einsum(
        "irpd,ripd->rpi",
        grad_all.reshape(total_rows, 2, pair_count, HEAD_SIZE),
        output_all,
        preferred_element_type=jnp.float32,
    ).reshape(pair_count, 2, total_rows)
    lse_all = row_logsumexp.reshape(pair_count, 2, total_rows)

    def tile(block_q, block_k, query_grad, kv_acc):
        offsets = jnp.arange(row_halves, dtype=jnp.int32)
        query_pos = block_q * row_halves + offsets
        key_pos = block_k * row_halves + offsets
        query_rows = lax.dynamic_slice_in_dim(
            query_all, block_q * row_halves, row_halves, 0
        ).reshape(row_halves, pair_count, 2, HEAD_SIZE)
        grad_rows = lax.dynamic_slice_in_dim(grad_all, block_q * row_halves, row_halves, 0).reshape(
            row_halves, pair_count, 2, HEAD_SIZE
        )
        key_rows = lax.dynamic_slice_in_dim(key_all, block_k * row_halves, row_halves, 0).reshape(
            row_halves, kv_count, HEAD_SIZE
        )
        value_rows = lax.dynamic_slice_in_dim(
            value_all, block_k * row_halves, row_halves, 0
        ).reshape(row_halves, kv_count, HEAD_SIZE)
        if head_count >= 4:
            key_rows = jnp.repeat(key_rows, 2, axis=1)
            value_rows = jnp.repeat(value_rows, 2, axis=1)
        lse_rows = lax.dynamic_slice_in_dim(lse_all, block_q * row_halves, row_halves, 2)
        delta_rows = lax.dynamic_slice_in_dim(delta_all, block_q * row_halves, row_halves, 2)
        query_docs = lax.dynamic_slice_in_dim(documents, block_q * row_halves, row_halves, 0)
        key_docs = lax.dynamic_slice_in_dim(documents, block_k * row_halves, row_halves, 0)
        allowed = (query_docs[:, None] == key_docs[None, :]) & (
            key_pos[None, :] <= query_pos[:, None]
        )
        scores = (
            jnp.einsum("qphd,cpd->phqc", query_rows, key_rows, preferred_element_type=jnp.float32)
            * score_scale
        )
        probs = jnp.exp(jnp.where(allowed, scores - lse_rows[..., None], -jnp.inf))
        probs_low = probs.astype(jnp.bfloat16)
        value_grad = jnp.einsum(
            "phqc,qphd->cpd", probs_low, grad_rows, preferred_element_type=jnp.float32
        )
        prob_grad = jnp.einsum(
            "qphd,cpd->phqc", grad_rows, value_rows, preferred_element_type=jnp.float32
        )
        score_grad = (probs * (prob_grad - delta_rows[..., None]) * score_scale).astype(
            jnp.bfloat16
        )
        query_tile = jnp.einsum(
            "phqc,cpd->qphd", score_grad, key_rows, preferred_element_type=jnp.float32
        )
        query_grad = query_grad + query_tile.reshape(row_halves, head_count * HEAD_SIZE)
        key_grad = jnp.einsum(
            "phqc,qphd->cpd", score_grad, query_rows, preferred_element_type=jnp.float32
        )
        tile_kv = jnp.concatenate([key_grad, value_grad], axis=2).reshape(
            row_halves, pair_count * 2 * HEAD_SIZE
        )
        target = block_k % 2 * wide_count + block_k // 2
        current = lax.dynamic_index_in_dim(kv_acc, target, 0, keepdims=False)
        kv_acc = lax.dynamic_update_index_in_dim(kv_acc, current + tile_kv, target, 0)
        return (query_grad, kv_acc)

    def empty_side():
        return (
            jnp.zeros((block_count, row_halves, head_count * HEAD_SIZE), jnp.float32),
            jnp.zeros((block_count, row_halves, pair_count * 2 * HEAD_SIZE), jnp.float32),
        )

    def attend_side():
        own_row = lax.dynamic_index_in_dim(tasks, wide_pos, 0, keepdims=False)

        def slot_turn(number, carry):
            query_acc, kv_acc = carry
            block_q = own_row[number, 0]
            valid = block_q >= 0
            safe_q = jnp.maximum(block_q, 0)
            upper = jnp.where(valid, safe_q + 1, 0)
            lower = jnp.where(valid, own_row[number, 1], 0)

            def key_turn(block_k, inner):
                return tile(safe_q, block_k, inner[0], inner[1])

            start = jnp.zeros((row_halves, head_count * HEAD_SIZE), jnp.float32)
            query_grad, kv_acc = lax.fori_loop(lower, upper, key_turn, (start, kv_acc))
            target = safe_q % 2 * wide_count + safe_q // 2
            current = lax.dynamic_index_in_dim(query_acc, target, 0, keepdims=False)
            query_acc = lax.dynamic_update_index_in_dim(query_acc, current + query_grad, target, 0)
            return (query_acc, kv_acc)

        return lax.fori_loop(0, block_count, slot_turn, empty_side())

    query_acc, kv_acc = lax.cond(is_worker, empty_side, attend_side)
    kv_flat = kv_acc.reshape(block_count * row_halves, pair_count * 2 * HEAD_SIZE)
    kv_sum = lax.psum_scatter(
        kv_flat.astype(jnp.bfloat16), ("role", "wide"), scatter_dimension=0, tiled=True
    )
    arrived = lax.all_to_all(
        query_acc.astype(jnp.bfloat16), ("role", "wide"), split_axis=0, concat_axis=0, tiled=True
    )
    query_piece = jnp.sum(arrived.astype(jnp.float32), axis=0).astype(jnp.bfloat16)
    head_q, key_value_head = (
        lax.all_gather(query_piece, ("role", "tp"), axis=1, tiled=True),
        lax.all_gather(kv_sum, ("role", "tp"), axis=1, tiled=True),
    )
    query_grads = head_q.reshape(row_halves, 2, QUERY_HEADS * HEAD_SIZE)
    grouped_queries = jnp.sum(
        key_value_head.reshape(row_halves, 2, KEY_VALUE_HEADS, 2, 2 * HEAD_SIZE).astype(
            jnp.float32
        ),
        axis=3,
    ).astype(jnp.bfloat16)
    key_gradients = grouped_queries[..., :HEAD_SIZE].reshape(
        row_halves, 2, KEY_VALUE_HEADS * HEAD_SIZE
    )
    value_gradients = grouped_queries[..., HEAD_SIZE:].reshape(
        row_halves, 2, KEY_VALUE_HEADS * HEAD_SIZE
    )
    qkv_grads = jnp.concatenate([query_grads, key_gradients, value_gradients], axis=2)
    normed_grad = jnp.einsum(
        "irc,nc->rin", qkv_grads, qkv_weight, preferred_element_type=jnp.float32
    )
    normed_grad = normed_grad.reshape(local_rows, qkv_weight.shape[0]).astype(jnp.bfloat16)
    qkv_part = jnp.einsum(
        "rin,irc->nc",
        normed.reshape(2, row_halves, normed.shape[1]),
        qkv_grads,
        preferred_element_type=jnp.float32,
    )
    out_sum, qkv_sum = (
        lax.psum_scatter(
            out_part.astype(jnp.bfloat16), "wide", scatter_dimension=1, tiled=True
        ).astype(jnp.float32),
        lax.psum_scatter(
            qkv_part.astype(jnp.bfloat16), "wide", scatter_dimension=1, tiled=True
        ).astype(jnp.float32),
    )
    return (normed_grad, out_sum.astype(jnp.bfloat16), qkv_sum.astype(jnp.bfloat16))


def solution(mesh):
    in_specs = (
        P("wide", ("role", "tp")),
        P("wide", "tp"),
        P("wide", None),
        P("wide", None),
        P("wide", "tp"),
        P("tp", None),
        P("wide", ("role", "tp")),
        P("tp", None),
        P(("role", "tp"), None),
        P(),
        P(),
    )
    out_specs = (P("wide", ("role", "tp")), P("tp", ("role", "wide")), P(("role", "tp"), "wide"))
    return jax.shard_map(local, mesh=mesh, in_specs=in_specs, out_specs=out_specs, check_vma=False)
```

profile of v0, /device:TPU:0, one launch (start us, length us, event | category | flops | bytes accessed | tf_op | source)
XLA Modules:
  0.0 686.1 jit_solution(5662846886879194408)
XLA Ops:
  7.2 0.0 copy-start
  7.2 0.0 all-gather.7.cloned.1.call-start
  7.2 1.3 copy.122
  8.5 0.0 all-gather.7.cloned.1.call-update
  8.6 0.0 all-gather.11.cloned.1.call-start
  8.6 0.1 copy-done
  8.7 0.8 constant_dynamic-slice_fusion.11
  9.5 0.0 all-gather.11.cloned.1.call-update
  9.6 0.0 all-gather.9.cloned.1.call-start
  9.6 49.6 %all-gather.7.cloned.1.call-done = bf16[512,4096]{1,0:T(8,128)(2,1)} async-done(((bf16[512,512]{1,0:T(8,128)(2,1)}), bf16[512,4096]{1,0:T(8,128)(2,1)}) %all-gather.7.cloned.1.call-update) | async-done | bytes 4194320 | tf_op jit(solution)/shard_map/all_gather | solution.py:38
  59.2 9.2 %conditional.2 = (bf16[512,1024]{1,0:T(8,128)(2,1)S(1)}) conditional(s32[]{:T(128)} %convert_element_type.57, (bf16[512,1024]{1,0:T(8,128)(2,1)S(1)}) %tuple.68, (bf16[512,4096]{1,0:T(8,128)(2,1)}, bf16[1024,4096]{1,0:T(8,128)(2,1)}) %tuple.64), branch_computations={%region_0.0_spmd, %region_1.0_spmd} | conditional | flops 4295491584 | bytes 13631496 | solution.py:52
  59.2 9.2 %convolution_convert_fusion = bf16[512,1024]{1,0:T(8,128)(2,1)S(1)} fusion(bf16[512,4096]{1,0:T(8,128)(2,1)} %get-tuple-element.517, bf16[1024,4096]{1,0:T(8,128)(2,1)} %get-tuple-element.570), kind=kOutput, calls=%fused_computation | convolution fusion | flops 4295491584 | bytes 13631488 | tf_op jit(solution)/shard_map/cond/branch_1_fun/dot_general | solution.py:45
  68.4 1.3 copy.54
  69.7 0.0 all-gather.9.cloned.1.call-update
  69.7 0.0 all-gather.13.cloned.1.call-start
  69.8 1.1 constant_dynamic-slice_fusion.9
  70.9 0.1 copy.91
  71.0 0.1 copy.90
  71.2 0.7 broadcast_select_fusion
  71.9 0.0 all-gather.13.cloned.1.call-update
  71.9 0.0 reduce-scatter.4.cloned.1.call-start
  72.0 25.1 %all-gather.11.cloned.1.call-done = bf16[4096,512]{1,0:T(8,128)(2,1)} async-done(((bf16[512,512]{1,0:T(8,128)(2,1)}), bf16[4096,512]{1,0:T(8,128)(2,1)}) %all-gather.11.cloned.1.call-update) | async-done | bytes 4194320 | tf_op jit(solution)/shard_map/all_gather | solution.py:63
  97.1 6.9 %reshape.119 = bf16[2,2048,4,128]{3,2,1,0:T(4,128)(2,1)} reshape(bf16[4096,512]{1,0:T(8,128)(2,1)} %all-gather.11.cloned.1.call-done) | data formatting | bytes 8388608 | tf_op jit(solution)/shard_map/reshape | solution.py:69
  104.0 6.3 bitcast_convert_fusion.1
  110.3 45.1 %all-gather.9.cloned.1.call-done = bf16[4096,1024]{0,1:T(8,128)(2,1)} async-done(((bf16[512,1024]{0,1:T(8,128)(2,1)}), bf16[4096,1024]{0,1:T(8,128)(2,1)}) %all-gather.9.cloned.1.call-update) | async-done | bytes 8388624 | tf_op jit(solution)/shard_map/all_gather | solution.py:61
  155.4 2.5 slice.30
  158.0 2.0 copy-done.1
  159.9 4.3 convert.2
  164.2 21.7 %all-gather.13.cloned.1.call-done = bf16[4096,256]{0,1:T(8,128)(2,1)} async-done(((bf16[512,256]{0,1:T(8,128)(2,1)}), bf16[4096,256]{0,1:T(8,128)(2,1)}) %all-gather.13.cloned.1.call-update) | async-done | bytes 2097168 | tf_op jit(solution)/shard_map/all_gather | solution.py:62
  185.9 7.9 %conditional.3 = (f32[8,256,1024]{1,2,0:T(8,128)}, f32[8,256,1024]{1,2,0:T(8,128)}) conditional(s32[]{:T(128)} %convert_element_type.57, (s32[]{:T(128)}, s32[4,8,2]{1,2,0:T(2,128)}, s32[2048]{0:T(1024)}, bf16[4096,1024]{0,1:T(8,128)(2,1)}, f32[8,2048]{1,0:T(8,128)S(1)}, /*index=5*/bf16[2048,1024]{0,1:T(8,128)(2,1)}, ...), branch_computations={%region_2.7_spmd.clone, %region_7.8_spmd} | conditional | flops 680706560 | bytes 96333480 | solution.py:163
  185.9 4.0 broadcast.49.clone
  189.9 4.0 broadcast.49
  193.8 7.3 %copy.57 = bf16[8,256,1024]{2,1,0:T(8,128)(2,1)} copy(f32[8,256,1024]{1,2,0:T(8,128)} %get-tuple-element.565) | data formatting | bytes 12582912 | tf_op jit(solution)/shard_map/cond | solution.py:163
  201.1 0.0 reduce-scatter.4.cloned.1.call-update
  201.1 0.0 all-gather.15.cloned.1.call-start
  201.1 3.8 convert_element_type.58
  205.0 240.8 %all_to_all.5 = bf16[8,256,1024]{1,2,0:T(8,128)(2,1)} all-to-all(bf16[8,256,1024]{1,2,0:T(8,128)(2,1)S(1)} %convert_element_type.58), channel_id=1, replica_groups=mesh['role'=2,'wide'=4,'tp'=4] {'role','wide'}, dimensions={0} | all-to-all | bytes 8388608 | tf_op jit(solution)/shard_map/all_to_all | solution.py:168
  445.8 3.7 reduce_sum.24
  449.5 0.0 all-gather.15.cloned.1.call-update
  449.5 0.0 all-gather.17.cloned.1.call-start
  449.6 3.7 reduce-scatter.4.cloned.1.call-done
  453.3 0.0 all-gather.17.cloned.1.call-update
  453.3 0.0 reduce-scatter.6.cloned.1.call-start
  453.4 6.0 convert_bitcast_fusion
  459.4 0.0 reduce-scatter.6.cloned.1.call-update
  459.5 0.3 reduce-scatter.8.cloned.1.call-start
  459.7 42.5 %all-gather.15.cloned.1.call-done = bf16[256,8192]{0,1:T(8,128)(2,1)} async-done(((bf16[256,1024]{0,1:T(8,128)(2,1)}), bf16[256,8192]{0,1:T(8,128)(2,1)}) %all-gather.15.cloned.1.call-update) | async-done | bytes 4194320 | tf_op jit(solution)/shard_map/all_gather | solution.py:173
  502.2 6.3 copy.60
  508.6 41.0 %all-gather.17.cloned.1.call-done = bf16[256,8192]{1,0:T(8,128)(2,1)} async-done(((bf16[256,1024]{1,0:T(8,128)(2,1)}), bf16[256,8192]{1,0:T(8,128)(2,1)}) %all-gather.17.cloned.1.call-update) | async-done | bytes 4194320 | tf_op jit(solution)/shard_map/all_gather | solution.py:174
  549.5 7.8 %reshape.122 = bf16[256,2,8,2,256]{4,3,2,1,0:T(2,128)(2,1)} reshape(bf16[256,8192]{1,0:T(8,128)(2,1)} %all-gather.17.cloned.1.call-done) | data formatting | bytes 8388608 | tf_op jit(solution)/shard_map/reshape | solution.py:178
  557.3 11.6 %reduce_sum.25 = bf16[256,2,8,256]{3,2,1,0:T(8,128)(2,1)S(1)} reduce(bf16[256,2,8,2,256]{4,3,2,1,0:T(2,128)(2,1)} %reshape.122, bf16[]{:T(256)} %constant.263.clone.1), dimensions={3}, to_apply=%region_10.11 | reduce | flops 1048576 | bytes 6291458 | tf_op jit(solution)/shard_map/reduce_sum | solution.py:177
  568.9 1.7 fusion.16
  570.6 1.3 reshape.138
  571.9 0.3 copy.84
  572.2 1.5 reshape.139
  573.7 0.3 copy.85
  574.0 1.0 copy-done.2
  574.9 8.5 %fusion.6 = bf16[512,6144]{0,1:T(8,128)(2,1)} fusion(bf16[2,256,512]{2,1,0:T(8,128)(2,1)} %bitcast.171, bf16[256,2,1024]{2,0,1:T(8,128)(2,1)S(1)} %copy.85, bf16[256,2,1024]{2,0,1:T(8,128)(2,1)S(1)} %copy.84, bf16[256,2,4096]{2,0,1:T(8,128)(2,1)} %copy.60), kind=kOutput, calls=%fused_computation.32 | convolution fusion | flops 3243245568 | bytes 13107200 | tf_op jit(solution)/shard_map/rin,irc->nc/dot_general | solution.py:194
  583.5 0.0 reduce-scatter.8.cloned.1.call-update
  583.5 20.5 %reduce-scatter.6.cloned.1.call-done = bf16[1024,512]{0,1:T(8,128)(2,1)} async-done(((bf16[1024,2048]{0,1:T(8,128)(2,1)}), bf16[1024,512]{0,1:T(8,128)(2,1)}) %reduce-scatter.6.cloned.1.call-update) | async-done | bytes 1048592 | tf_op jit(solution)/shard_map/reduce_scatter | solution.py:201
  603.9 2.3 copy.62
  606.2 8.3 %fusion.10 = bf16[256,2,512]{2,0,1:T(8,128)(2,1)} fusion(bf16[512,6144]{1,0:T(8,128)(2,1)} %param.27, bf16[256,2,1024]{2,0,1:T(8,128)(2,1)S(1)} %copy-done.3, bf16[256,2,1024]{2,0,1:T(8,128)(2,1)S(1)} %copy.84, bf16[256,2,4096]{2,0,1:T(8,128)(2,1)} %copy.60), kind=kOutput, calls=%fused_computation.39 | convolution fusion | flops 3240361984 | bytes 13107200 | tf_op jit(solution)/shard_map/irc,nc->rin/dot_general | solution.py:190
  614.5 62.5 %reduce-scatter.8.cloned.1.call-done = bf16[512,1536]{0,1:T(8,128)(2,1)} async-done(((bf16[512,6144]{0,1:T(8,128)(2,1)}), bf16[512,1536]{0,1:T(8,128)(2,1)}) %reduce-scatter.8.cloned.1.call-update) | async-done | bytes 1572880 | tf_op jit(solution)/shard_map/reduce_scatter | solution.py:204
  677.0 2.6 copy.63
  (6 shorter events, 0.0 us)
Async XLA Ops:
  7.2 1.5 copy-start
  7.2 52.0 %all-gather.7.cloned.1.call-start = ((), (), s32[]{:S(2)}) async-start(), calls=%async_computation.4 | async-start | bytes 4718592 | tf_op jit(solution)/shard_map/all_gather | solution.py:38
  8.6 88.5 %all-gather.11.cloned.1.call-start = ((), (), s32[]{:S(2)}) async-start(), calls=%async_computation.6 | async-start | bytes 4718592 | tf_op jit(solution)/shard_map/all_gather | solution.py:63
  9.6 145.9 %all-gather.9.cloned.1.call-start = ((), (), s32[]{:S(2)}) async-start(), calls=%async_computation.5 | async-start | bytes 9437184 | tf_op jit(solution)/shard_map/all_gather | solution.py:61
  69.7 116.1 %all-gather.13.cloned.1.call-start = ((), (), s32[]{:S(2)}) async-start(), calls=%async_computation.7 | async-start | bytes 2359296 | tf_op jit(solution)/shard_map/all_gather | solution.py:62
  71.9 381.4 %reduce-scatter.4.cloned.1.call-start = ((), (), s32[]{:S(2)}) async-start(), calls=%async_computation.9 | async-start | bytes 4718592 | tf_op jit(solution)/shard_map/reduce_scatter | solution.py:165
  157.9 2.0 copy-start.1
  159.9 26.0 %copy-start.4 = (f32[8,2048]{1,0:T(8,128)S(1)}, f32[8,2048]{1,0:T(8,128)}, u32[]{:S(2)}) copy-start(f32[8,2048]{1,0:T(8,128)} %param.24) | copy-start | bytes 196612
  201.1 301.1 %all-gather.15.cloned.1.call-start = ((), (), s32[]{:S(2)}) async-start(), calls=%async_computation.8 | async-start | bytes 4718592 | tf_op jit(solution)/shard_map/all_gather | solution.py:173
  449.5 100.0 %all-gather.17.cloned.1.call-start = ((), (), s32[]{:S(2)}) async-start(), calls=%async_computation.10 | async-start | bytes 4718592 | tf_op jit(solution)/shard_map/all_gather | solution.py:174
  453.3 150.6 %reduce-scatter.6.cloned.1.call-start = ((), (), s32[]{:S(2)}) async-start(), calls=%async_computation.11 | async-start | bytes 5242880 | tf_op jit(solution)/shard_map/reduce_scatter | solution.py:201
  459.5 217.6 %reduce-scatter.8.cloned.1.call-start = ((), (), s32[]{:S(2)}) async-start(), calls=%async_computation.12 | async-start | bytes 7864320 | tf_op jit(solution)/shard_map/reduce_scatter | solution.py:204
  574.0 1.0 copy-start.2
  583.4 22.8 %copy-start.3 = (bf16[256,2,1024]{2,0,1:T(8,128)(2,1)S(1)}, bf16[256,2,1024]{2,0,1:T(8,128)(2,1)}, u32[]{:S(2)}) copy-start(bf16[256,2,1024]{2,0,1:T(8,128)(2,1)} %copy-done.2) | copy-start | bytes 3145732
Sparse Core Ops, SparseCore 0:
  9.6 49.5 all-gather.6
  61.7 35.3 all-gather.10
  99.5 55.8 all-gather.8
  157.8 28.0 all-gather.12
  201.2 252.0 reduce-scatter.3
  455.3 46.8 all-gather.14
  503.8 45.6 all-gather.16
  552.5 51.3 reduce-scatter.5
  606.9 70.0 reduce-scatter.7
where the time goes:
time: 690 us; the launch traced here: 686 us
  waiting for transfers between devices  312 us (45%)
  blocking collectives  241 us (35%)
  local copies, waits for them, and re-layouts  56.4 us (8%)
  matrix products  32 us (5%)
  other arithmetic  30.5 us (4%)
  between operations  14 us (2%)
    all_to_all x1, blocking collectives, local(): lax.all_to_all(query_acc.astype(jnp.bfloat16), ('role', 'wide'), split_ax...  241 us
    reduce_scatter x1, waiting for transfers between devices, local(): lax.psum_scatter(qkv_part.astype(jnp.bfloat16), 'wide', scatter_dimension...  62.5 us
    all_gather x1, waiting for transfers between devices, local(): full_grad = lax.all_gather(out_grad, ('role', 'tp'), axis=1, tiled=True)  49.6 us
    all_gather x1, waiting for transfers between devices, local(): lax.all_gather(first_piece, ('role', 'wide'), axis=0, tiled=True)  45.1 us
    all_gather x1, waiting for transfers between devices, local(): lax.all_gather(query_piece, ('role', 'tp'), axis=1, tiled=True)  42.5 us
    all_gather x1, waiting for transfers between devices, local(): lax.all_gather(kv_sum, ('role', 'tp'), axis=1, tiled=True)  41 us
    all_gather x1, waiting for transfers between devices, local(): lax.all_gather(out_piece, ('role', 'wide'), axis=0, tiled=True)  25.1 us
    all_gather x1, waiting for transfers between devices, local(): lax.all_gather(kv_piece, ('role', 'wide'), axis=0, tiled=True)  21.7 us
  transfers between devices with their start and end apart: 9, of which 9 were waited for; matrix products, arithmetic and copies ran while one was open for 14% of the time, Pallas kernels for 0%

commit v1 on v0

--- a/solution.py
+++ b/solution.py
@@ -7,6 +7,28 @@
 QUERY_HEADS = 32
 KEY_VALUE_HEADS = 8
 HEAD_SIZE = 128
+
+
+def in_order(blocks, dim):
+    shape = list(blocks.shape[1:])
+    shape[dim] *= blocks.shape[0]
+    return jnp.moveaxis(blocks, 0, dim).reshape(shape)
+
+
+def grow_blocks(shard, axis):
+    devices = lax.axis_size(axis)
+    blocks = shard[None]
+    for level in range(devices.bit_length() - 1):
+        stride = 1 << level
+        theirs = lax.ppermute(blocks, axis, [(i, i ^ stride) for i in range(devices)])
+        both = jnp.stack([blocks, theirs])
+        upper = lax.axis_index(axis) >> level & 1
+        blocks = jnp.where(upper == 0, both, both[::-1]).reshape(-1, *shard.shape)
+    return blocks
+
+
+def collect(array, axis, dim):
+    return in_order(grow_blocks(array, axis), dim)
 
 
 def local(
@@ -35,7 +57,7 @@
     score_scale = HEAD_SIZE ** (-0.5)
     total_rows = wide_count * local_rows
     block_count = tasks.shape[1]
-    full_grad = lax.all_gather(out_grad, ("role", "tp"), axis=1, tiled=True)
+    full_grad = collect(out_grad, ("role", "tp"), 1)
     grad_half = lax.dynamic_slice_in_dim(full_grad, role_pos * (D // 2), D // 2, 1)
     out_part = lax.dot_general(
         attn_out, grad_half, (((0,), (0,)), ((), ())), preferred_element_type=jnp.float32

time: 690 us -> 663 us (0.961)
  waiting for transfers between devices: 312 us -> 269 us
    ppermute x0 -> x3, waiting for transfers between devices: none -> 61.4 us  [grow_blocks(): lax.ppermute(blocks, axis, [(i, i ^ stride) for i in range(devices)])]
    all_gather x1 -> x0, waiting for transfers between devices: 49.6 us -> none  [local(): full_grad = lax.all_gather(out_grad, ('role', 'tp'), axis=1, tiled=True)]
    all_gather x1, waiting for transfers between devices: 25.1 us -> 0.02 us  [local(): lax.all_gather(out_piece, ('role', 'wide'), axis=0, tiled=True)]
    reduce_scatter x1, waiting for transfers between devices: 20.5 us -> 0.03 us  [local(): lax.psum_scatter(out_part.astype(jnp.bfloat16), 'wide', scatter_dimension...]
  transfers between devices with their start and end apart: 9 -> 11, of which waited for: 9 -> 9; matrix products, arithmetic and copies ran while one was open for 14% -> 16% of each run, Pallas kernels for 0% -> 0%
where the time goes in v1:
time: 663 us; the launch traced here: 659 us
  waiting for transfers between devices  269 us (41%)
  blocking collectives  240 us (36%)
  local copies, waits for them, and re-layouts  57.9 us (9%)
  other arithmetic  36.4 us (5%)
  matrix products  33.2 us (5%)
  between operations  15.8 us (2%)
    all_to_all x1, blocking collectives, local(): lax.all_to_all(query_acc.astype(jnp.bfloat16), ('role', 'wide'), split_ax...  240 us
    ppermute x3, waiting for transfers between devices, grow_blocks(): lax.ppermute(blocks, axis, [(i, i ^ stride) for i in range(devices)])  61.4 us
    reduce_scatter x1, waiting for transfers between devices, local(): lax.psum_scatter(qkv_part.astype(jnp.bfloat16), 'wide', scatter_dimension...  57.2 us
    all_gather x1, waiting for transfers between devices, local(): lax.all_gather(query_piece, ('role', 'tp'), axis=1, tiled=True)  42.5 us
    all_gather x1, waiting for transfers between devices, local(): lax.all_gather(first_piece, ('role', 'wide'), axis=0, tiled=True)  41.7 us
    all_gather x1, waiting for transfers between devices, local(): lax.all_gather(kv_sum, ('role', 'tp'), axis=1, tiled=True)  40.7 us
    all_gather x1, waiting for transfers between devices, local(): lax.all_gather(kv_piece, ('role', 'wide'), axis=0, tiled=True)  21.8 us
  transfers between devices with their start and end apart: 11, of which 9 were waited for; matrix products, arithmetic and copies ran while one was open for 16% of the time, Pallas kernels for 0%

profile of v1, /device:TPU:0, one launch (start us, length us, event | category | flops | bytes accessed | tf_op | source)
XLA Modules:
  0.0 658.8 jit_solution(8647721238110526426)
XLA Ops:
  8.0 0.0 all-gather.8.cloned.1.call-start
  8.1 1.2 copy-done
  9.2 0.8 constant_dynamic-slice_fusion.11
  10.1 0.0 all-gather.6.cloned.1.call-start
  10.1 3.1 collective-permute-start
  13.2 12.1 %collective-permute-done = bf16[1,512,512]{2,1,0:T(8,128)(2,1)S(1)} collective-permute-done((bf16[1,512,512]{2,1,0:T(8,128)(2,1)}, bf16[1,512,512]{2,1,0:T(8,128)(2,1)S(1)}, u32[]{:S(2)}, u32[]{:S(2)}) %collective-permute-start) | collective-permute-done | bytes 524320 | tf_op jit(solution)/shard_map/ppermute | solution.py:23
  25.4 1.1 pad_maximum_fusion.8
  26.5 0.3 fusion.14
  26.8 2.8 collective-permute-start.1
  29.6 45.0 %collective-permute-done.1 = bf16[2,512,512]{2,1,0:T(8,128)(2,1)} collective-permute-done((bf16[2,512,512]{2,1,0:T(8,128)(2,1)S(1)}, bf16[2,512,512]{2,1,0:T(8,128)(2,1)}, u32[]{:S(2)}, u32[]{:S(2)}) %collective-permute-start.1) | collective-permute-done | bytes 1048608 | tf_op jit(solution)/shard_map/ppermute | solution.py:23
  74.6 1.4 pad_maximum_fusion.5
  76.1 0.4 reverse_select_fusion.1
  76.5 0.1 collective-permute-start.2
  76.6 4.3 collective-permute-done.2
  80.9 2.0 pad_maximum_fusion.2
  82.8 0.9 reverse_select_fusion
  83.8 2.6 copy.96
  86.3 9.2 %conditional.2 = (bf16[512,1024]{1,0:T(8,128)(2,1)S(1)}) conditional(s32[]{:T(128)} %convert_element_type.57, (bf16[512,1024]{1,0:T(8,128)(2,1)S(1)}) %tuple.144, (bf16[512,4096]{1,0:T(8,128)(2,1)}, bf16[1024,4096]{1,0:T(8,128)(2,1)}) %tuple.143), branch_computations={%region_0.1_spmd, %region_1.2_spmd} | conditional | flops 4295491584 | bytes 13631496 | solution.py:74
  86.3 9.2 %convolution_convert_fusion = bf16[512,1024]{1,0:T(8,128)(2,1)S(1)} fusion(bf16[512,4096]{1,0:T(8,128)(2,1)} %get-tuple-element.517, bf16[1024,4096]{1,0:T(8,128)(2,1)} %get-tuple-element.570), kind=kOutput, calls=%fused_computation | convolution fusion | flops 4295491584 | bytes 13631488 | tf_op jit(solution)/shard_map/cond/branch_1_fun/dot_general | solution.py:67
  95.5 1.3 copy.57
  96.9 0.0 all-gather.10.cloned.1.call-start
  96.9 1.1 constant_dynamic-slice_fusion.9
  98.0 0.1 copy.95
  98.2 0.1 copy.94
  98.3 0.7 broadcast_select_fusion
  99.1 0.0 reduce-scatter.4.cloned.1.call-start
  99.1 0.0 all-gather.8.cloned.1.call-done
  99.2 7.0 %reshape.135 = bf16[2,2048,4,128]{3,2,1,0:T(4,128)(2,1)} reshape(bf16[4096,512]{1,0:T(8,128)(2,1)} %all-gather.8.cloned.1.call-done) | data formatting | bytes 8388608 | tf_op jit(solution)/shard_map/reshape | solution.py:91
  106.2 6.2 bitcast_convert_fusion.1
  112.4 41.7 %all-gather.6.cloned.1.call-done = bf16[4096,1024]{0,1:T(8,128)(2,1)} async-done(((bf16[512,1024]{0,1:T(8,128)(2,1)}), bf16[4096,1024]{0,1:T(8,128)(2,1)}) %all-gather.6.cloned.1.call-update) | async-done | bytes 8388624 | tf_op jit(solution)/shard_map/all_gather | solution.py:83
  154.0 2.5 slice.30
  156.5 1.9 copy-done.1
  158.5 4.3 convert.2
  162.8 21.8 %all-gather.10.cloned.1.call-done = bf16[4096,256]{0,1:T(8,128)(2,1)} async-done(((bf16[512,256]{0,1:T(8,128)(2,1)}), bf16[4096,256]{0,1:T(8,128)(2,1)}) %all-gather.10.cloned.1.call-update) | async-done | bytes 2097168 | tf_op jit(solution)/shard_map/all_gather | solution.py:84
  184.6 7.9 %conditional.3 = (f32[8,256,1024]{1,2,0:T(8,128)}, f32[8,256,1024]{1,2,0:T(8,128)}) conditional(s32[]{:T(128)} %convert_element_type.57, (s32[]{:T(128)}, s32[4,8,2]{1,2,0:T(2,128)}, s32[2048]{0:T(1024)}, bf16[4096,1024]{0,1:T(8,128)(2,1)}, f32[8,2048]{1,0:T(8,128)S(1)}, /*index=5*/bf16[2048,1024]{0,1:T(8,128)(2,1)}, ...), branch_computations={%region_2.7_spmd.clone, %region_7.8_spmd} | conditional | flops 680706560 | bytes 96333480 | solution.py:185
  184.6 4.0 broadcast.49.clone
  188.6 4.0 broadcast.49
  192.5 7.3 %copy.60 = bf16[8,256,1024]{2,1,0:T(8,128)(2,1)} copy(f32[8,256,1024]{1,2,0:T(8,128)} %get-tuple-element.565) | data formatting | bytes 12582912 | tf_op jit(solution)/shard_map/cond | solution.py:185
  199.8 0.0 all-gather.12.cloned.1.call-start
  199.9 3.8 convert_element_type.58
  203.7 239.7 %all_to_all.5 = bf16[8,256,1024]{1,2,0:T(8,128)(2,1)} all-to-all(bf16[8,256,1024]{1,2,0:T(8,128)(2,1)S(1)} %convert_element_type.58), channel_id=1, replica_groups=mesh['role'=2,'wide'=4,'tp'=4] {'role','wide'}, dimensions={0} | all-to-all | bytes 8388608 | tf_op jit(solution)/shard_map/all_to_all | solution.py:190
  443.4 3.7 reduce_sum.24
  447.1 0.0 all-gather.14.cloned.1.call-start
  447.2 3.7 reduce-scatter.4.cloned.1.call-done
  451.0 0.0 reduce-scatter.6.cloned.1.call-start
  451.0 6.0 convert_bitcast_fusion
  457.0 0.0 reduce-scatter.6.cloned.1.call-update
  457.1 0.3 reduce-scatter.8.cloned.1.call-start
  457.3 42.5 %all-gather.12.cloned.1.call-done = bf16[256,8192]{0,1:T(8,128)(2,1)} async-done(((bf16[256,1024]{0,1:T(8,128)(2,1)}), bf16[256,8192]{0,1:T(8,128)(2,1)}) %all-gather.12.cloned.1.call-update) | async-done | bytes 4194320 | tf_op jit(solution)/shard_map/all_gather | solution.py:195
  499.8 6.4 copy.63
  506.3 40.7 %all-gather.14.cloned.1.call-done = bf16[256,8192]{1,0:T(8,128)(2,1)} async-done(((bf16[256,1024]{1,0:T(8,128)(2,1)}), bf16[256,8192]{1,0:T(8,128)(2,1)}) %all-gather.14.cloned.1.call-update) | async-done | bytes 4194320 | tf_op jit(solution)/shard_map/all_gather | solution.py:196
  547.0 7.8 %reshape.138 = bf16[256,2,8,2,256]{4,3,2,1,0:T(2,128)(2,1)} reshape(bf16[256,8192]{1,0:T(8,128)(2,1)} %all-gather.14.cloned.1.call-done) | data formatting | bytes 8388608 | tf_op jit(solution)/shard_map/reshape | solution.py:200
  554.8 11.4 %reduce_sum.25 = bf16[256,2,8,256]{3,2,1,0:T(8,128)(2,1)S(1)} reduce(bf16[256,2,8,2,256]{4,3,2,1,0:T(2,128)(2,1)} %reshape.138, bf16[]{:T(256)} %constant.266.clone.1), dimensions={3}, to_apply=%region_10.11 | reduce | flops 1048576 | bytes 6291458 | tf_op jit(solution)/shard_map/reduce_sum | solution.py:199
  566.2 1.7 fusion.18
  567.9 1.4 reshape.154
  569.3 1.3 copy.88
  570.6 0.3 reshape.155
  570.9 0.3 copy.89
  571.2 8.7 %fusion.6 = bf16[512,6144]{0,1:T(8,128)(2,1)} fusion(bf16[2,256,512]{2,1,0:T(8,128)(2,1)} %bitcast.196, bf16[256,2,1024]{2,0,1:T(8,128)(2,1)S(1)} %copy.89, bf16[256,2,1024]{2,0,1:T(8,128)(2,1)} %copy.88, bf16[256,2,4096]{2,0,1:T(8,128)(2,1)} %copy.63), kind=kOutput, calls=%fused_computation.32 | convolution fusion | flops 3243245568 | bytes 13107200 | tf_op jit(solution)/shard_map/rin,irc->nc/dot_general | solution.py:216
  579.9 0.0 reduce-scatter.6.cloned.1.call-done
  580.0 2.4 copy.65
  582.3 9.3 %fusion.10 = bf16[256,2,512]{2,0,1:T(8,128)(2,1)} fusion(bf16[512,6144]{1,0:T(8,128)(2,1)} %param.27, bf16[256,2,1024]{2,0,1:T(8,128)(2,1)S(1)} %copy.89, bf16[256,2,1024]{2,0,1:T(8,128)(2,1)S(1)} %copy-done.4, bf16[256,2,4096]{2,0,1:T(8,128)(2,1)} %copy.63), kind=kOutput, calls=%fused_computation.44 | convolution fusion | flops 3240361984 | bytes 13107200 | tf_op jit(solution)/shard_map/irc,nc->rin/dot_general | solution.py:212
  591.6 57.2 %reduce-scatter.8.cloned.1.call-done = bf16[512,1536]{0,1:T(8,128)(2,1)} async-done(((bf16[512,6144]{0,1:T(8,128)(2,1)}), bf16[512,1536]{0,1:T(8,128)(2,1)}) %reduce-scatter.8.cloned.1.call-update) | async-done | bytes 1572880 | tf_op jit(solution)/shard_map/reduce_scatter | solution.py:226
  648.8 2.6 copy.66
  (17 shorter events, 0.1 us)
Async XLA Ops:
  8.0 1.2 copy-start
  8.0 91.1 %all-gather.8.cloned.1.call-start = ((), (), s32[]{:S(2)}) async-start(), calls=%async_computation.5 | async-start | bytes 4718592 | tf_op jit(solution)/shard_map/all_gather | solution.py:85
  10.1 143.9 %all-gather.6.cloned.1.call-start = ((), (), s32[]{:S(2)}) async-start(), calls=%async_computation.4 | async-start | bytes 9437184 | tf_op jit(solution)/shard_map/all_gather | solution.py:83
  10.1 15.3 %collective-permute-start = (bf16[1,512,512]{2,1,0:T(8,128)(2,1)}, bf16[1,512,512]{2,1,0:T(8,128)(2,1)S(1)}, u32[]{:S(2)}, u32[]{:S(2)}) collective-permute-start(bf16[1,512,512]{2,1,0:T(8,128)(2,1)} %bitcast.193), channel_id=1, source_target_pairs={{0,1},{1,0},{2,3},{3,2},{16,17},{17,16},{18,19},{19,18},{4,5},{5,4... | collective-permute-start | bytes 1572872 | tf_op jit(solution)/shard_map/ppermute | solution.py:23
  26.8 47.9 %collective-permute-start.1 = (bf16[2,512,512]{2,1,0:T(8,128)(2,1)S(1)}, bf16[2,512,512]{2,1,0:T(8,128)(2,1)}, u32[]{:S(2)}, u32[]{:S(2)}) collective-permute-start(bf16[2,512,512]{2,1,0:T(8,128)(2,1)S(1)} %get-tuple-element.689), channel_id=1, source_target_pairs={{0,2},{1,3},{2,0},{3,1},{16,18},{17,19},{18,16},{19,17},{4,6},{5,7... | collective-permute-start | bytes 3145736 | tf_op jit(solution)/shard_map/ppermute | solution.py:23
  76.5 4.4 collective-permute-start.2
  83.8 2.6 copy-start.2
  96.9 87.7 %all-gather.10.cloned.1.call-start = ((), (), s32[]{:S(2)}) async-start(), calls=%async_computation.6 | async-start | bytes 2359296 | tf_op jit(solution)/shard_map/all_gather | solution.py:84
  99.1 351.9 %reduce-scatter.4.cloned.1.call-start = ((), (), s32[]{:S(2)}) async-start(), calls=%async_computation.8 | async-start | bytes 4718592 | tf_op jit(solution)/shard_map/reduce_scatter | solution.py:187
  156.5 2.0 copy-start.1
  158.5 26.1 %copy-start.5 = (f32[8,2048]{1,0:T(8,128)S(1)}, f32[8,2048]{1,0:T(8,128)}, u32[]{:S(2)}) copy-start(f32[8,2048]{1,0:T(8,128)} %param.24) | copy-start | bytes 196612
  199.8 300.0 %all-gather.12.cloned.1.call-start = ((), (), s32[]{:S(2)}) async-start(), calls=%async_computation.7 | async-start | bytes 4718592 | tf_op jit(solution)/shard_map/all_gather | solution.py:195
  447.1 99.9 %all-gather.14.cloned.1.call-start = ((), (), s32[]{:S(2)}) async-start(), calls=%async_computation.9 | async-start | bytes 4718592 | tf_op jit(solution)/shard_map/all_gather | solution.py:196
  451.0 129.0 %reduce-scatter.6.cloned.1.call-start = ((), (), s32[]{:S(2)}) async-start(), calls=%async_computation.10 | async-start | bytes 5242880 | tf_op jit(solution)/shard_map/reduce_scatter | solution.py:223
  457.1 191.7 %reduce-scatter.8.cloned.1.call-start = ((), (), s32[]{:S(2)}) async-start(), calls=%async_computation.11 | async-start | bytes 7864320 | tf_op jit(solution)/shard_map/reduce_scatter | solution.py:226
  567.9 2.7 copy-start.3
  579.9 2.4 copy-start.4
Sparse Core Ops, SparseCore 0:
  11.3 39.2 all-gather.7
  97.0 56.9 all-gather.5
  156.5 28.0 all-gather.9
  199.9 250.9 reduce-scatter.3
  452.9 46.8 all-gather.11
  501.3 45.6 all-gather.13
Sparse Core Ops, SparseCore 1:
  457.1 52.5 reduce-scatter.5
  580.0 68.7 reduce-scatter.7
